TPU v7x, 32 devices: a whole 2x2x4 slice. The times are simulated.
32 devices in a mesh: groups: 2 (over y), lanes: 4 (over z), heads: 2 (over x), rep: 2 (over core).
Axes of the slice: x: 2, y: 2, z: 4, core: 2. Of those that a mesh axis runs over, the one named last changes fastest.
Arguments:
- queries: bfloat16 [4096, 2048], P(('groups', 'lanes'), ('heads', 'rep')), parts along dimension 0, may hold values from -6 to 6
- span_states: bfloat16 [4096, 896], P(('groups', 'lanes')), parts along dimension 0, may hold values from -6 to 6
- store: bfloat16 [128, 128, 896], P(('groups', 'lanes'), ('heads', 'rep')), parts along dimension 0, may hold values from -480 to 480
- entry_ids: int32 [64, 2], P(('groups', 'lanes')), parts along dimension 0, may hold values from 0 to 15
- owners: int32 [64, 2], P(('groups', 'lanes')), parts along dimension 0, may hold values from 0 to 3, as said below
- w_key: bfloat16 [896, 2048], P(None, ('heads', 'rep')), may hold values from -0.1875 to 0.1875
- w_value: bfloat16 [896, 2048], P(None, ('heads', 'rep')), may hold values from -0.1875 to 0.1875
- w_out: bfloat16 [2048, 4096], P(('heads', 'rep')), may hold values from -0.125 to 0.125
Outputs:
- attended: bfloat16 [4096, 4096], P(('groups', 'lanes', 'heads', 'rep')), parts along dimension 0
There are 2 independent parts, one for each index of `groups`. A program takes and returns all parts, laid end to end along the dimension named above; an argument that names none is the same for every part. Nothing has to cross between parts.
Inputs may be any that keep to these rules, and one draw needn't show every extreme that they name: Among the 16 neighbours of one lane's spans at most 4 have the same owner, the 2 owners of a span differ, and in every draw one owner holds 4 neighbours of every lane.
All inputs are finite; a program needn't handle non-finite values.
Results may differ from a plain program's by a relative error of at most 0.014.
The roundings to bfloat16 on the way count: a program that leaves them out, or rounds other values in their place, can miss the bound.
Values may be sent and summed in bfloat16 or wider, within the bound.
A program may use at most 128 MiB of HBM per device.

v0:
```python
import functools

import jax
import jax.numpy as jnp
from jax import lax
from jax.experimental import pallas as pl
from jax.experimental.pallas import tpu as pltpu
from jax.sharding import PartitionSpec as P

HD = 128
ENCODER_HEAD_DIM = 128
MESH = pl.DeviceIdType.MESH
F32 = jnp.float32
BF16 = jnp.bfloat16


def softmax_parts(parts):
    top = functools.reduce(jnp.maximum, [jnp.max(p, axis=-1, keepdims=True) for p in parts])
    exps = [jnp.exp(p - top) for p in parts]
    total = functools.reduce(jnp.add, [jnp.sum(e, axis=-1, keepdims=True) for e in exps])
    inv = 1.0 / total
    return [(e * inv).astype(BF16) for e in exps]


def dot_t(a, b):
    return lax.dot_general(a, b, (((1,), (1,)), ((), ())), preferred_element_type=F32)


def fused(
    n_lanes, n_x, n_c, cap, n_cols,
    owner_ref, entry_ref, query_hbm, states_hbm, store_hbm, wk_hbm, wv_hbm, wo_hbm,
    out_ref,
    query_v, states_v, store_v, wk_v, wv_v, wo_v,
    table, span_table, span_sm, own_sm, got_sm, rank_sm,
    send_tok, recv_tok, enc, keys, values, heads_out,
    part, part_in, summed, summed_in,
    load_sem, local_sem, idx_send, idx_recv, tok_sends, tok_recvs, x_sends, c_sends, enc_recvs,
    part_send, part_recv, sum_send, sum_recv,
):
    lane = lax.axis_index("lanes")
    x = lax.axis_index("heads")
    c = lax.axis_index("rep")
    mate = n_c - 1 - c
    fanout, spans = owner_ref.shape
    requests = spans * fanout
    width = store_v.shape[2]
    span_len = query_v.shape[1]
    chip_spans = spans // n_x
    col = wo_v.shape[1] // n_cols
    quarter = x * n_c + c

    loads = [
        pltpu.make_async_copy(src, dst, load_sem.at[i])
        for i, (src, dst) in enumerate(
            (
                (store_hbm, store_v),
                (states_hbm, states_v),
                (wk_hbm, wk_v),
                (wv_hbm, wv_v),
                (query_hbm, query_v),
                (wo_hbm, wo_v),
            )
        )
    ]
    for load in loads[:2]:
        load.start()

    barrier = pltpu.get_barrier_semaphore()
    for d in range(1, n_lanes):
        pl.semaphore_signal(barrier, inc=1, device_id={"lanes": lax.rem(lane + d, n_lanes)}, device_id_type=MESH)
    for d in range(1, n_x):
        pl.semaphore_signal(barrier, inc=1, device_id={"heads": lax.rem(x + d, n_x)}, device_id_type=MESH)
    pl.semaphore_signal(barrier, inc=1, device_id={"rep": mate}, device_id_type=MESH)

    owner = [owner_ref[j % fanout, j // fanout] for j in range(requests)]
    order = [
        (j // fanout % chip_spans * n_x + j // fanout // chip_spans) * fanout + j % fanout for j in range(requests)
    ]
    place = lax.broadcasted_iota(jnp.int32, table.shape, 1)
    entries = jnp.zeros(table.shape, jnp.int32)
    whose = jnp.zeros(table.shape, jnp.int32)
    for j in range(requests):
        rank = jnp.int32(0)
        for i in range(requests):
            if order[i] < order[j]:
                rank = rank + (owner[i] == owner[j]).astype(jnp.int32)
        rank_sm[j] = jnp.minimum(rank, cap - 1)
        hit = place == owner[j] * cap + rank
        entries = jnp.where(hit, entry_ref[j % fanout, j // fanout], entries)
        whose = jnp.where(hit, j // fanout, whose)
    table[...] = entries
    span_table[...] = whose
    pl.semaphore_wait(barrier, n_lanes + n_x - 1)

    def idx_copy(d):
        return pltpu.make_async_remote_copy(
            src_ref=table, dst_ref=got_sm.at[lane], send_sem=idx_send.at[d], recv_sem=idx_recv.at[d],
            device_id={"lanes": lax.rem(lane + d, n_lanes)}, device_id_type=MESH,
        )

    for d in range(1, n_lanes):
        idx_copy(d).start()
    to_sm = pltpu.make_async_copy(span_table, span_sm, local_sem.at[0])
    to_sm.start()
    own_to_sm = pltpu.make_async_copy(table, own_sm, local_sem.at[1])
    own_to_sm.start()
    to_sm.wait()
    own_to_sm.wait()
    loads[0].wait()
    loads[1].wait()
    for load in loads[2:]:
        load.start()

    def tok_copy(r, d):
        return pltpu.make_async_remote_copy(
            src_ref=send_tok.at[r, d], dst_ref=recv_tok.at[r, d],
            send_sem=tok_sends.at[r, d], recv_sem=tok_recvs.at[r, d],
            device_id={"lanes": lax.rem(lane + d, n_lanes)}, device_id_type=MESH,
        )

    def send_one(r, d):
        who = lax.rem(lane + d, n_lanes)
        send_tok[r, d] = store_v[got_sm[who, 0, lane * cap + r]]
        tok_copy(r, d).start()

    def send_rank(r, carry):
        def one(d, carry):
            send_one(r, d)
            return carry

        return lax.fori_loop(1, n_lanes, one, carry)

    def x_copy(r, s, d):
        return pltpu.make_async_remote_copy(
            src_ref=enc.at[r, s, quarter], dst_ref=enc.at[r, s, quarter],
            send_sem=x_sends.at[r, s, d], recv_sem=enc_recvs.at[r, s, quarter],
            device_id={"heads": lax.rem(x + d, n_x)}, device_id_type=MESH,
        )

    def c_copy(r, s, block):
        return pltpu.make_async_remote_copy(
            src_ref=enc.at[r, s, block], dst_ref=enc.at[r, s, block],
            send_sem=c_sends.at[r, s, block // n_c], recv_sem=enc_recvs.at[r, s, block],
            device_id={"rep": mate}, device_id_type=MESH,
        )

    def arrived(r, s, block):
        pltpu.make_async_remote_copy(
            src_ref=enc.at[r, s, block], dst_ref=enc.at[r, s, block],
            send_sem=c_sends.at[r, s, block // n_c], recv_sem=enc_recvs.at[r, s, block],
            device_id={"rep": mate}, device_id_type=MESH,
        ).wait_recv()

    def source(d):
        return lax.rem(lane - d + n_lanes, n_lanes)

    def encode(group, fetch):
        tokens = [fetch(r, d) for r, d in group]
        states = [states_v[span_sm[0, source(d) * cap + r]] for r, d in group]
        heads = [
            (n, slice(h * ENCODER_HEAD_DIM, (h + 1) * ENCODER_HEAD_DIM))
            for n in range(len(group))
            for h in range(width // ENCODER_HEAD_DIM)
        ]
        logits = [dot_t(tokens[n][:, cols], states[n][:, cols]) * ENCODER_HEAD_DIM ** (-0.5) for n, cols in heads]
        weights = [softmax_parts([logit])[0] for logit in logits]
        mixed = [
            jnp.dot(weight, states[n][:, cols], preferred_element_type=F32) for weight, (n, cols) in zip(weights, heads)
        ]
        for mix, (n, cols) in zip(mixed, heads):
            r, d = group[n]
            enc[r, source(d), quarter, :, cols] = (tokens[n][:, cols].astype(F32) + mix).astype(BF16)
        for r, d in group:
            s = source(d)
            for k in range(1, n_x):
                x_copy(r, s, k).start()
            c_copy(r, s, quarter).start()

    def relay(group):
        for k in range(1, n_x):
            block = lax.rem(x + k, n_x) * n_c + c
            for r, d in group:
                arrived(r, source(d), block)
                c_copy(r, source(d), block).start()

    here = [(r, 0) for r in range(cap)]
    encode(here, lambda r, d: store_v[own_sm[0, lane * cap + r]])
    for d in sorted(range(1, n_lanes), key=lambda d: min(d, n_lanes - d)):
        idx_copy(d).wait_recv()
        send_one(0, n_lanes - d)
    lax.fori_loop(1, cap, send_rank, 0)
    groups = n_lanes - 1
    lag = min(3, groups)

    def members(i):
        r, g = i // groups, i % groups
        return [(r, 1 + g)]

    lane_chunk = min(n_lanes, 4)

    def project(r):
        def chunk(g, carry):
            def settle(s, carry):
                for k in range(n_x):
                    arrived(r, g * lane_chunk + s, k * n_c + mate)
                return carry

            lax.fori_loop(0, lane_chunk, settle, 0)
            some = pl.ds(g * lane_chunk, lane_chunk)
            rows = enc[r, some].reshape(-1, width)
            for weight, target in ((wk_v, keys), (wv_v, values)):
                result = jnp.dot(rows, weight[...], preferred_element_type=F32).astype(BF16)
                target[r, some] = result.reshape((lane_chunk,) + target.shape[2:])
            return carry

        lax.fori_loop(0, n_lanes // lane_chunk, chunk, 0)

    def attend(first, i, count):
        slots = [
            [(rank_sm[(first + n) * fanout + f], owner_ref[f, first + n]) for f in range(fanout)] for n in range(count)
        ]
        heads = [
            (n, slice(h * HD, (h + 1) * HD)) for n in range(count) for h in range(query_v.shape[2] // HD)
        ]
        logits = [
            [dot_t(query_v[first + n, :, cols], keys[r, o, :, cols]) * HD ** (-0.5) for r, o in slots[n]]
            for n, cols in heads
        ]
        weights = [softmax_parts(parts) for parts in logits]
        mixed = [
            functools.reduce(
                jnp.add,
                [
                    jnp.dot(w, values[r, o, :, cols], preferred_element_type=F32)
                    for w, (r, o) in zip(parts, slots[n])
                ],
            )
            for parts, (n, cols) in zip(weights, heads)
        ]
        for mix, (n, cols) in zip(mixed, heads):
            heads_out[i + n, :, cols] = mix.astype(BF16)

    def part_copy(k, j, n):
        return pltpu.make_async_remote_copy(
            src_ref=part.at[k, j, mate, n], dst_ref=part_in.at[k, j, n],
            send_sem=part_send.at[k, j, n], recv_sem=part_recv.at[k, j, n],
            device_id={"rep": mate}, device_id_type=MESH,
        )

    def sum_copy(k, j, n):
        return pltpu.make_async_remote_copy(
            src_ref=summed.at[k, j, n], dst_ref=summed_in.at[k, j, n],
            send_sem=sum_send.at[k, j, n], recv_sem=sum_recv.at[k, j, n],
            device_id={"heads": lax.rem(x + k + 1, n_x)}, device_id_type=MESH,
        )

    def columns(j):
        return pl.ds(pl.multiple_of(j * col, col), col)

    together = max(t for t in (1, 2, 4) if chip_spans % t == 0)
    core_spans = chip_spans // n_c

    def early(k, n, core):
        return jnp.logical_and(core == 0, k < n_x - 1) if n == 0 else False

    def combine(k, j, n):
        part_copy(k, j, n).wait_recv()
        both = part[k, j, c, n].astype(F32) + part_in[k, j, n].astype(F32)
        summed[k, j, n] = both.astype(BF16)
        sum_copy(k, j, n).start()

    def early_parts():
        loads[4].wait()
        loads[5].wait()
        for k in range(n_x - 1):
            attend(lax.rem(x + k + 1, n_x) * chip_spans, 0, 1)
            rows = heads_out[0]

            def step(j, carry):
                part[k, j, 0, 0] = jnp.dot(rows, wo_v[:, columns(j)], preferred_element_type=F32).astype(BF16)

                @pl.when(mate == 0)
                def _():
                    part_copy(k, j, 0).start()

                return carry

            lax.fori_loop(0, n_cols, step, 0)

    def early_sums():
        for k in range(n_x - 1):

            def step(j, carry):
                combine(k, j, 0)
                return carry

            @pl.when(c == 0)
            def _():
                lax.fori_loop(0, n_cols, step, 0)

    early_turn = min(n_x, cap)

    def turn(r, carry):
        def slot(g, carry):
            i = r * groups + g

            @pl.when(r < cap)
            def _():
                for member in members(i):
                    tok_copy(*member).wait_recv()
                encode(members(i), lambda r, d: recv_tok[r, d])

            @pl.when(i == lag - 1)
            def _():
                relay(here)

            @pl.when(jnp.logical_and(i >= lag, i < cap * groups + lag))
            def _():
                relay(members(i - lag))

            return carry

        lax.fori_loop(0, groups, slot, 0)

        @pl.when(r == 1)
        def _():
            loads[2].wait()
            loads[3].wait()

        if early_turn <= cap - 2:
            @pl.when(r == cap - 1)
            def _():
                early_sums()

        @pl.when(r >= 1)
        def _():
            project(r - 1)

        @pl.when(r == early_turn)
        def _():
            early_parts()
            if early_turn > cap - 2:
                early_sums()

        return carry

    lax.fori_loop(0, cap + 1, turn, 0)
    def chip(k, carry):
        def some_spans(i, carry):
            attend(lax.rem(x + k + 1, n_x) * chip_spans + i * together, i * together, together)
            return carry

        lax.fori_loop(0, chip_spans // together, some_spans, 0)
        rows = heads_out[...].reshape(-1, heads_out.shape[2])

        def step(j, carry):
            @pl.when(j < n_cols)
            def _():
                result = jnp.dot(rows, wo_v[:, columns(j)], preferred_element_type=F32).astype(BF16)
                result = result.reshape(part.shape[2:])
                for core in range(n_c):
                    for n in range(core_spans):

                        @pl.when(jnp.logical_not(early(k, n, core)))
                        def _():
                            part[k, j, core, n] = result[core, n]

                for n in range(core_spans):

                    @pl.when(jnp.logical_not(early(k, n, mate)))
                    def _():
                        part_copy(k, j, n).start()

            @pl.when(jnp.logical_and(j >= 1, k < n_x - 1))
            def _():
                for n in range(core_spans):

                    @pl.when(jnp.logical_not(early(k, n, c)))
                    def _():
                        combine(k, j - 1, n)

            return carry

        return lax.fori_loop(0, n_cols + 1, step, carry)

    lax.fori_loop(0, n_x, chip, 0)

    def finish(j, carry):
        for n in range(core_spans):
            part_copy(n_x - 1, j, n).wait_recv()
            total = part[n_x - 1, j, c, n].astype(F32) + part_in[n_x - 1, j, n].astype(F32)
            for k in range(n_x - 1):
                sum_copy(k, j, n).wait_recv()
                total = total + summed_in[k, j, n].astype(F32)
            out_ref[n * span_len : (n + 1) * span_len, columns(j)] = total.astype(BF16)
        return carry

    lax.fori_loop(0, n_cols, finish, 0)

    for d in range(1, n_lanes):
        idx_copy(d).wait_send()

    def drain(i, carry):
        r, d = i // n_lanes, i % n_lanes

        @pl.when(d > 0)
        def _():
            tok_copy(r, d).wait_send()

        for k in range(1, n_x):
            x_copy(r, d, k).wait_send()
        for k in range(n_x):
            c_copy(r, d, k * n_c + c).wait_send()
        return carry

    lax.fori_loop(0, cap * n_lanes, drain, 0)

    def drain_out(j, carry):
        for k in range(n_x):
            for n in range(core_spans):
                part_copy(k, j, n).wait_send()
                if k < n_x - 1:
                    sum_copy(k, j, n).wait_send()
        return carry

    lax.fori_loop(0, n_cols, drain_out, 0)


def shards(queries, span_states, store, entry_ids, owners, w_key, w_value, w_out):
    n_lanes, n_x, n_c = (lax.axis_size(name) for name in ("lanes", "heads", "rep"))
    spans, fanout = entry_ids.shape
    requests = spans * fanout
    cap = max(2, (requests + n_lanes - 1) // n_lanes)
    span_len = queries.shape[0] // spans
    tok_dev, width = store.shape[1:]
    tokens = tok_dev * n_x * n_c
    head_cols, model = w_out.shape
    out_rows = queries.shape[0] // (n_x * n_c)
    n_cols = 4
    core_spans = spans // (n_x * n_c)
    col = model // n_cols
    lanes_wide = -(-(n_lanes * cap) // 128) * 128
    dma = pltpu.SemaphoreType.DMA
    hbm = pl.BlockSpec(memory_space=pl.ANY)
    smem = pl.BlockSpec(memory_space=pltpu.SMEM)
    return pl.pallas_call(
        functools.partial(fused, n_lanes, n_x, n_c, cap, n_cols),
        out_shape=pltpu.VMEM((out_rows, model), BF16),
        in_specs=[smem, smem] + [hbm] * 6,
        out_specs=pl.BlockSpec(memory_space=pltpu.VMEM),
        scratch_shapes=[
            pltpu.VMEM((spans, span_len, head_cols), BF16),
            pltpu.VMEM((spans, span_len, width), BF16),
            pltpu.VMEM(store.shape, BF16),
            pltpu.VMEM(w_key.shape, BF16),
            pltpu.VMEM(w_value.shape, BF16),
            pltpu.VMEM(w_out.shape, BF16),
            pltpu.VMEM((8, lanes_wide), jnp.int32),
            pltpu.VMEM((8, lanes_wide), jnp.int32),
            pltpu.SMEM((8, lanes_wide), jnp.int32),
            pltpu.SMEM((8, lanes_wide), jnp.int32),
            pltpu.SMEM((n_lanes, 8, lanes_wide), jnp.int32),
            pltpu.SMEM((requests,), jnp.int32),
            pltpu.VMEM((cap, n_lanes, tok_dev, width), BF16),
            pltpu.VMEM((cap, n_lanes, tok_dev, width), BF16),
            pltpu.VMEM((cap, n_lanes, n_x * n_c, tok_dev, width), BF16),
            pltpu.VMEM((cap, n_lanes, tokens, head_cols), BF16),
            pltpu.VMEM((cap, n_lanes, tokens, head_cols), BF16),
            pltpu.VMEM((spans // n_x, span_len, head_cols), BF16),
            pltpu.VMEM((n_x, n_cols, n_c, core_spans, span_len, col), BF16),
            pltpu.VMEM((n_x, n_cols, core_spans, span_len, col), BF16),
            pltpu.VMEM((n_x, n_cols, core_spans, span_len, col), BF16),
            pltpu.VMEM((n_x, n_cols, core_spans, span_len, col), BF16),
            dma((6,)),
            dma((2,)),
            dma((n_lanes,)),
            dma((n_lanes,)),
            dma((cap, n_lanes)),
            dma((cap, n_lanes)),
            dma((cap, n_lanes, n_x)),
            dma((cap, n_lanes, n_x)),
            dma((cap, n_lanes, n_x * n_c)),
            dma((n_x, n_cols, core_spans)),
            dma((n_x, n_cols, core_spans)),
            dma((n_x, n_cols, core_spans)),
            dma((n_x, n_cols, core_spans)),
        ],
        compiler_params=pltpu.CompilerParams(
            collective_id=0, has_side_effects=True, vmem_limit_bytes=60000000
        ),
    )(
        owners.T,
        entry_ids.T,
        queries.reshape(spans, span_len, head_cols),
        span_states.reshape(spans, span_len, width),
        store,
        w_key,
        w_value,
        w_out,
    )


def solution(mesh):
    return jax.shard_map(
        shards,
        mesh=mesh,
        in_specs=(
            P(("groups", "lanes"), ("heads", "rep")),
            P(("groups", "lanes"), None),
            P(("groups", "lanes"), ("heads", "rep"), None),
            P(("groups", "lanes"), None),
            P(("groups", "lanes"), None),
            P(None, ("heads", "rep")),
            P(None, ("heads", "rep")),
            P(("heads", "rep"), None),
        ),
        out_specs=P(("groups", "lanes", "heads", "rep"), None),
        check_vma=False,
    )
```

profile of v0, /device:TPU:1, one launch (start us, length us, event | category | flops | bytes accessed | tf_op | source)
XLA Modules:
  0.0 66.5 jit_solution(2814061692687299995)
XLA Ops:
  0.0 65.5 %shard_map.82 = bf16[128,4096]{1,0:T(8,128)(2,1)S(1)} custom-call(s32[2,8]{1,0:T(2,128)} %bitcast.6, s32[2,8]{1,0:T(2,128)} %bitcast.7, bf16[8,64,512]{2,1,0:T(8,128)(2,1)} %bitcast.5, bf16[8,64,896]{2,1,0:T(8,128)(2,1)} %bitcast.4, bf16[16,32,896]{2,1,0:T(8,128)(2,1)} %store_hbm.1, bf16[896,512]{1,0:T(8,128)(2,1)} %wk_hbm.1, bf16[896,512]{1,0:T(8,128)(2,1)} %wv_hbm.1, ...), custom_call_target="tpu_custom_call" | custom-call | tf_op jit(solution)/shard_map/pallas_call | solution.py:446
  65.5 1.0 %copy.10 = bf16[128,4096]{1,0:T(8,128)(2,1)} copy(bf16[128,4096]{1,0:T(8,128)(2,1)S(1)} %shard_map.82) | data formatting | bytes 2097152
where the time goes:
time: 66.7 us; the launch traced here: 66.5 us
  Pallas kernels  65.5 us (98%)
  local copies, waits for them, and re-layouts  0.97 us (1%)
    pallas_call x1, Pallas kernels, shards(): pl.pallas_call(functools.partial(fused, n_lanes, n_x, n_c, cap, n_cols),...  65.5 us

commit v1 on v0

v1 whole, which is shorter than its diff:
```python
import functools
import itertools

import jax
import jax.numpy as jnp
from jax import lax
from jax.experimental import pallas as pl
from jax.experimental.pallas import tpu as pltpu
from jax.sharding import PartitionSpec as P

HD = 128
ENCODER_HEAD_DIM = 128
MESH = pl.DeviceIdType.MESH
F32 = jnp.float32
BF16 = jnp.bfloat16


def softmax_parts(parts):
    top = functools.reduce(jnp.maximum, [jnp.max(p, axis=-1, keepdims=True) for p in parts])
    exps = [jnp.exp(p - top) for p in parts]
    total = functools.reduce(jnp.add, [jnp.sum(e, axis=-1, keepdims=True) for e in exps])
    inv = 1.0 / total
    return [(e * inv).astype(BF16) for e in exps]


def dot_t(a, b):
    return lax.dot_general(a, b, (((1,), (1,)), ((), ())), preferred_element_type=F32)


def early_spans(n_x, n_lanes, cap, spans, fanout):
    whole = n_x == 2 and cap == n_lanes == 4 and fanout == 2 and spans == 2 * n_lanes
    return spans // n_x // 2 if whole else 0


def fused(
    n_lanes, n_x, n_c, cap, n_cols,
    owner_ref, entry_ref, query_hbm, states_hbm, store_hbm, wk_hbm, wv_hbm, wo_hbm,
    out_ref,
    query_v, states_v, store_v, wk_v, wv_v, wo_v,
    table, span_table, span_sm, own_sm, got_sm, rank_sm, virtual_sm, slot_sm,
    send_tok, recv_tok, enc, keys, values, heads_out,
    part, part_in, summed, summed_in, final, final_out,
    load_sem, local_sem, idx_send, idx_recv, tok_sends, tok_recvs, x_send, c_send, x_recvs, c_recvs,
    part_send, part_recv, sum_send, sum_recv, final_send, final_recv,
):
    lane = lax.axis_index("lanes")
    x = lax.axis_index("heads")
    c = lax.axis_index("rep")
    mate = n_c - 1 - c
    fanout, spans = owner_ref.shape
    requests = spans * fanout
    width = store_v.shape[2]
    span_len = query_v.shape[1]
    chip_spans = spans // n_x
    core_spans = chip_spans // n_c
    col = wo_v.shape[1] // n_cols
    half = span_len // n_c
    quarter = x * n_c + c
    early = early_spans(n_x, n_lanes, cap, spans, fanout)
    stages = part.shape[1]
    batch = chip_spans // stages

    loads = [
        pltpu.make_async_copy(src, dst, load_sem.at[i])
        for i, (src, dst) in enumerate(
            (
                (store_hbm, store_v),
                (states_hbm, states_v),
                (wk_hbm, wk_v),
                (wv_hbm, wv_v),
                (query_hbm, query_v),
                (wo_hbm, wo_v),
            )
        )
    ]
    for load in loads[:2]:
        load.start()

    barrier = pltpu.get_barrier_semaphore()
    for d in range(1, n_lanes):
        pl.semaphore_signal(barrier, inc=1, device_id={"lanes": lax.rem(lane + d, n_lanes)}, device_id_type=MESH)
    for d in range(1, n_x):
        pl.semaphore_signal(barrier, inc=1, device_id={"heads": lax.rem(x + d, n_x)}, device_id_type=MESH)
    pl.semaphore_signal(barrier, inc=1, device_id={"rep": mate}, device_id_type=MESH)

    owner = [owner_ref[j % fanout, j // fanout] for j in range(requests)]
    ranks = []
    if early:
        word = [
            sum(jnp.where(owner[s * fanout + f] == o, 1 << (4 * o), 0) for f in range(fanout) for o in range(n_lanes))
            for s in range(spans)
        ]
        target = sum((cap // 2) << (4 * o) for o in range(n_lanes))
        chosen = list(itertools.combinations(range(chip_spans), early))
        sums = [[sum(word[h * chip_spans + s] for s in some) for some in chosen] for h in range(n_x)]
        mask = jnp.int32(0)
        for a, some in enumerate(chosen):
            for b, others in enumerate(chosen):
                bits = sum(1 << s for s in some) + sum(1 << (chip_spans + s) for s in others)
                mask = jnp.where(sums[0][a] + sums[1][b] == target, bits, mask)
        first, later = jnp.int32(0), jnp.int32(target)
        slot = []
        for s in range(spans):
            if s % chip_spans == 0:
                n_first, n_later = jnp.int32(0), jnp.int32(early)
            taken = ((mask >> s) & 1) == 1
            ahead = jnp.where(taken, first, later)
            for f in range(fanout):
                ranks.append(
                    sum(jnp.where(owner[s * fanout + f] == o, (ahead >> (4 * o)) & 15, 0) for o in range(n_lanes))
                )
            first, later = first + jnp.where(taken, word[s], 0), later + jnp.where(taken, 0, word[s])
            slot.append(jnp.where(taken, n_first, n_later))
            n_first, n_later = n_first + jnp.where(taken, 1, 0), n_later + jnp.where(taken, 0, 1)
        for s in range(spans):
            base = s // chip_spans * chip_spans
            slot_sm[s] = jnp.minimum(slot[s], chip_spans - 1)
            virtual_sm[s] = sum(jnp.where(slot[base + i] == s - base, base + i, 0) for i in range(chip_spans))
    else:
        for j in range(requests):
            ranks.append(sum((owner[i] == owner[j]).astype(jnp.int32) for i in range(j)) + jnp.int32(0))
        for s in range(spans):
            slot_sm[s] = s % chip_spans
            virtual_sm[s] = s
    place = lax.broadcasted_iota(jnp.int32, table.shape, 1)
    entries = jnp.zeros(table.shape, jnp.int32)
    whose = jnp.zeros(table.shape, jnp.int32)
    for j, rank in enumerate(ranks):
        rank_sm[j] = jnp.minimum(rank, cap - 1)
        hit = place == owner[j] * cap + rank
        entries = jnp.where(hit, entry_ref[j % fanout, j // fanout], entries)
        whose = jnp.where(hit, j // fanout, whose)
    table[...] = entries
    span_table[...] = whose
    pl.semaphore_wait(barrier, n_lanes + n_x - 1)

    def idx_copy(d):
        return pltpu.make_async_remote_copy(
            src_ref=table, dst_ref=got_sm.at[lane], send_sem=idx_send.at[d], recv_sem=idx_recv.at[d],
            device_id={"lanes": lax.rem(lane + d, n_lanes)}, device_id_type=MESH,
        )

    for d in range(1, n_lanes):
        idx_copy(d).start()
    to_sm = pltpu.make_async_copy(span_table, span_sm, local_sem.at[0])
    to_sm.start()
    own_to_sm = pltpu.make_async_copy(table, own_sm, local_sem.at[1])
    own_to_sm.start()
    to_sm.wait()
    own_to_sm.wait()
    loads[0].wait()
    loads[1].wait()
    for load in loads[2:]:
        load.start()

    def tok_copy(r, d):
        return pltpu.make_async_remote_copy(
            src_ref=send_tok.at[r, d], dst_ref=recv_tok.at[r, d],
            send_sem=tok_sends.at[r], recv_sem=tok_recvs.at[r, d],
            device_id={"lanes": lax.rem(lane + d, n_lanes)}, device_id_type=MESH,
        )

    def sent(ref, sem):
        pltpu.make_async_remote_copy(
            src_ref=ref, dst_ref=ref, send_sem=sem, recv_sem=sem, device_id={"rep": mate}, device_id_type=MESH
        ).wait_send()

    def toks_sent(r):
        sent(send_tok.at[r, pl.ds(1, n_lanes - 1)], tok_sends.at[r])

    def send_one(r, d):
        who = lax.rem(lane + d, n_lanes)
        send_tok[r, d] = store_v[got_sm[who, 0, lane * cap + r]]
        tok_copy(r, d).start()

    def send_rank(r):
        def one(d, carry):
            send_one(r, d)
            return carry

        lax.fori_loop(1, n_lanes, one, 0)

    def x_copy(r, s, d):
        return pltpu.make_async_remote_copy(
            src_ref=enc.at[r, s, quarter], dst_ref=enc.at[r, s, quarter],
            send_sem=x_send.at[0], recv_sem=x_recvs.at[r, s, d - 1],
            device_id={"heads": lax.rem(x + d, n_x)}, device_id_type=MESH,
        )

    def c_copy(r, s, block):
        return pltpu.make_async_remote_copy(
            src_ref=enc.at[r, s, block], dst_ref=enc.at[r, s, block],
            send_sem=c_send.at[0], recv_sem=c_recvs.at[r],
            device_id={"rep": mate}, device_id_type=MESH,
        )

    def source(d):
        return lax.rem(lane - d + n_lanes, n_lanes)

    def encode(group, fetch):
        tokens = [fetch(r, d) for r, d in group]
        states = [states_v[span_sm[0, source(d) * cap + r]] for r, d in group]
        heads = [
            (n, slice(h * ENCODER_HEAD_DIM, (h + 1) * ENCODER_HEAD_DIM))
            for n in range(len(group))
            for h in range(width // ENCODER_HEAD_DIM)
        ]
        logits = [dot_t(tokens[n][:, cols], states[n][:, cols]) * ENCODER_HEAD_DIM ** (-0.5) for n, cols in heads]
        weights = [softmax_parts([logit])[0] for logit in logits]
        mixed = [
            jnp.dot(weight, states[n][:, cols], preferred_element_type=F32) for weight, (n, cols) in zip(weights, heads)
        ]
        for mix, (n, cols) in zip(mixed, heads):
            r, d = group[n]
            enc[r, source(d), quarter, :, cols] = (tokens[n][:, cols].astype(F32) + mix).astype(BF16)
        for r, d in group:
            s = source(d)
            for k in range(1, n_x):
                x_copy(r, s, k).start()
            c_copy(r, s, quarter).start()

    def relay(r, d):
        s = source(d)
        for k in range(1, n_x):
            block = lax.rem(x - k + n_x, n_x) * n_c + c
            pltpu.make_async_remote_copy(
                src_ref=enc.at[r, s, block], dst_ref=enc.at[r, s, block],
                send_sem=x_send.at[0], recv_sem=x_recvs.at[r, s, k - 1],
                device_id={"rep": mate}, device_id_type=MESH,
            ).wait_recv()
            c_copy(r, s, block).start()

    encode([(r, 0) for r in range(cap)], lambda r, d: store_v[own_sm[0, lane * cap + r]])
    ahead = min(2, cap)
    for d in sorted(range(1, n_lanes), key=lambda d: min(d, n_lanes - d)):
        idx_copy(d).wait_recv()
        send_one(0, n_lanes - d)
    for r in range(1, ahead):
        send_rank(r)
    groups = n_lanes - 1
    total = cap * groups
    lag = min(2, groups)
    lane_chunk = min(n_lanes, 4)

    def settle(r):
        ref = enc.at[r, :, pl.ds(0, n_x)]
        pltpu.make_async_remote_copy(
            src_ref=ref, dst_ref=ref, send_sem=c_send.at[0], recv_sem=c_recvs.at[r],
            device_id={"rep": mate}, device_id_type=MESH,
        ).wait_recv()

    def project(r):
        settle(r)

        def chunk(g, carry):
            some = pl.ds(g * lane_chunk, lane_chunk)
            rows = enc[r, some].reshape(-1, width)
            for weight, target in ((wk_v, keys), (wv_v, values)):
                result = jnp.dot(rows, weight[...], preferred_element_type=F32).astype(BF16)
                target[r, some] = result.reshape((lane_chunk,) + target.shape[2:])
            return carry

        lax.fori_loop(0, n_lanes // lane_chunk, chunk, 0)

    def attend(k, e):
        first = lax.rem(x + k + 1, n_x) * chip_spans + e * batch
        which = [virtual_sm[first + n] for n in range(batch)]
        slots = [[(rank_sm[s * fanout + f], owner_ref[f, s]) for f in range(fanout)] for s in which]
        heads = [(n, slice(h * HD, (h + 1) * HD)) for n in range(batch) for h in range(query_v.shape[2] // HD)]
        logits = [
            [dot_t(query_v[which[n], :, cols], keys[r, o, :, cols]) * HD ** (-0.5) for r, o in slots[n]]
            for n, cols in heads
        ]
        weights = [softmax_parts(parts) for parts in logits]
        mixed = [
            functools.reduce(
                jnp.add,
                [
                    jnp.dot(w, values[r, o, :, cols], preferred_element_type=F32)
                    for w, (r, o) in zip(parts, slots[n])
                ],
            )
            for parts, (n, cols) in zip(weights, heads)
        ]
        for mix, (n, cols) in zip(mixed, heads):
            heads_out[n, :, cols] = mix.astype(BF16)

    def part_copy(k, e, j):
        return pltpu.make_async_remote_copy(
            src_ref=part.at[k, e, j, mate], dst_ref=part_in.at[k, e, j],
            send_sem=part_send.at[0], recv_sem=part_recv.at[k, e, j],
            device_id={"rep": mate}, device_id_type=MESH,
        )

    def sum_copy(k, e, j):
        return pltpu.make_async_remote_copy(
            src_ref=summed.at[k, e, j], dst_ref=summed_in.at[k, e, j],
            send_sem=sum_send.at[0], recv_sem=sum_recv.at[k, e, j],
            device_id={"heads": lax.rem(x + k + 1, n_x)}, device_id_type=MESH,
        )

    def columns(j):
        return pl.ds(pl.multiple_of(j * col, col), col)

    def product(k, e, j):
        rows = heads_out[...].reshape(-1, heads_out.shape[2])
        result = jnp.dot(rows, wo_v[:, columns(j)], preferred_element_type=F32).astype(BF16)
        result = result.reshape((batch, n_c, half, col))
        for core in range(n_c):
            for n in range(batch):
                part[k, e, j, core, n] = result[n, core]
        part_copy(k, e, j).start()

    def combine(k, e, j):
        part_copy(k, e, j).wait_recv()
        both = part[k, e, j, c].astype(F32) + part_in[k, e, j].astype(F32)
        summed[k, e, j] = both.astype(BF16)
        sum_copy(k, e, j).start()

    def products(k, e):
        attend(k, e)

        def step(j, carry):
            product(k, e, j)
            return carry

        lax.fori_loop(0, n_cols, step, 0)

    def combines(k, e, lo, hi):
        def step(j, carry):
            combine(k, e, j)
            return carry

        lax.fori_loop(lo, hi, step, 0)

    own = n_x - 1
    ready = cap // 2 - 1

    def slot_step(i, carry):
        r, d = i // groups, 1 + i % groups
        tok_copy(r, d).wait_recv()
        encode([(r, d)], lambda r, d: recv_tok[r, d])

        @pl.when(i == lag - 1)
        def _():
            for n in range(cap):
                relay(n, 0)

        @pl.when(i >= lag)
        def _():
            relay((i - lag) // groups, 1 + (i - lag) % groups)

        for n in range(ahead, cap):

            @pl.when(i == (n - 1) * groups - 1)
            def _():
                toks_sent(n - ahead)
                send_rank(n)

        @pl.when(i == groups + lag - 1)
        def _():
            loads[2].wait()
            loads[3].wait()

        for n in range(cap - 1):

            @pl.when(i == (n + 1) * groups + lag - 1)
            def _():
                project(n)
                if early and n == ready:
                    loads[4].wait()
                    loads[5].wait()
                    for k in range(own):
                        products(k, 0)
                if early and n == ready + 1:
                    for k in range(own):
                        combines(k, 0, 1, 2)

        if early:

            @pl.when(i == (ready + 2) * groups)
            def _():
                for k in range(own):
                    combines(k, 0, 0, 1)

        return carry

    lax.fori_loop(0, total, slot_step, 0)
    if early:
        for k in range(own):
            combines(k, 0, 2, n_cols // 2)
        products(own, 0)
        for k in range(own):
            combines(k, 0, n_cols // 2, n_cols)
    else:
        loads[4].wait()
        loads[5].wait()

    def late_relay(i, carry):
        relay(i // groups, 1 + i % groups)
        return carry

    lax.fori_loop(total - lag, total, late_relay, 0)
    project(cap - 1)
    last = stages - 1
    behind = min(5, n_cols)
    for k in range(own):
        attend(k, last)

        def late(j, carry):
            @pl.when(j < n_cols)
            def _():
                product(k, last, j)

            @pl.when(j >= behind)
            def _():
                combine(k, last, j - behind)

            return carry

        lax.fori_loop(0, n_cols + behind, late, 0)
    products(own, last)

    def final_copy(j, n):
        rows = pl.ds(pl.multiple_of(n * span_len + c * half, half), half)
        return pltpu.make_async_remote_copy(
            src_ref=final_out.at[j, n], dst_ref=out_ref.at[rows, columns(j)],
            send_sem=final_send.at[0], recv_sem=final_recv.at[0],
            device_id={"rep": mate}, device_id_type=MESH,
        )

    def finish(j, carry):
        for e in range(stages):
            part_copy(own, e, j).wait_recv()
            total = part[own, e, j, c].astype(F32) + part_in[own, e, j].astype(F32)
            for k in range(own):
                sum_copy(k, e, j).wait_recv()
                total = total + summed_in[k, e, j].astype(F32)
            final[e * batch : (e + 1) * batch] = total.astype(BF16)
        for n in range(core_spans):
            first = x * chip_spans + n
            final_out[j, n] = final[slot_sm[first + mate * core_spans]]
            final_copy(j, n).start()
            rows = pl.ds(pl.multiple_of(n * span_len + c * half, half), half)
            out_ref[rows, columns(j)] = final[slot_sm[first + c * core_spans]]
        return carry

    lax.fori_loop(0, n_cols, finish, 0)
    for d in range(1, n_lanes):
        idx_copy(d).wait_send()
    for r in range(cap - ahead, cap):
        toks_sent(r)
    sent(enc.at[:, :, pl.ds(0, n_x - 1)], x_send.at[0])
    sent(enc.at[:, :, pl.ds(0, n_x)], c_send.at[0])
    sent(part_in, part_send.at[0])
    sent(summed, sum_send.at[0])
    sent(final_out, final_send.at[0])
    pltpu.make_async_remote_copy(
        src_ref=final_out, dst_ref=final_out, send_sem=final_send.at[0], recv_sem=final_recv.at[0],
        device_id={"rep": mate}, device_id_type=MESH,
    ).wait_recv()


def shards(queries, span_states, store, entry_ids, owners, w_key, w_value, w_out):
    n_lanes, n_x, n_c = (lax.axis_size(name) for name in ("lanes", "heads", "rep"))
    spans, fanout = entry_ids.shape
    requests = spans * fanout
    cap = max(2, (requests + n_lanes - 1) // n_lanes)
    span_len = queries.shape[0] // spans
    tok_dev, width = store.shape[1:]
    tokens = tok_dev * n_x * n_c
    head_cols, model = w_out.shape
    out_rows = queries.shape[0] // (n_x * n_c)
    n_cols = 8
    core_spans = spans // (n_x * n_c)
    chip_spans = spans // n_x
    stages = 2 if early_spans(n_x, n_lanes, cap, spans, fanout) else 1
    batch = chip_spans // stages
    half = span_len // n_c
    col = model // n_cols
    lanes_wide = -(-(n_lanes * cap) // 128) * 128
    dma = pltpu.SemaphoreType.DMA
    hbm = pl.BlockSpec(memory_space=pl.ANY)
    smem = pl.BlockSpec(memory_space=pltpu.SMEM)
    return pl.pallas_call(
        functools.partial(fused, n_lanes, n_x, n_c, cap, n_cols),
        out_shape=pltpu.VMEM((out_rows, model), BF16),
        in_specs=[smem, smem] + [hbm] * 6,
        out_specs=pl.BlockSpec(memory_space=pltpu.VMEM),
        scratch_shapes=[
            pltpu.VMEM((spans, span_len, head_cols), BF16),
            pltpu.VMEM((spans, span_len, width), BF16),
            pltpu.VMEM(store.shape, BF16),
            pltpu.VMEM(w_key.shape, BF16),
            pltpu.VMEM(w_value.shape, BF16),
            pltpu.VMEM(w_out.shape, BF16),
            pltpu.VMEM((8, lanes_wide), jnp.int32),
            pltpu.VMEM((8, lanes_wide), jnp.int32),
            pltpu.SMEM((8, lanes_wide), jnp.int32),
            pltpu.SMEM((8, lanes_wide), jnp.int32),
            pltpu.SMEM((n_lanes, 8, lanes_wide), jnp.int32),
            pltpu.SMEM((requests,), jnp.int32),
            pltpu.SMEM((spans,), jnp.int32),
            pltpu.SMEM((spans,), jnp.int32),
            pltpu.VMEM((cap, n_lanes, tok_dev, width), BF16),
            pltpu.VMEM((cap, n_lanes, tok_dev, width), BF16),
            pltpu.VMEM((cap, n_lanes, n_x * n_c, tok_dev, width), BF16),
            pltpu.VMEM((cap, n_lanes, tokens, head_cols), BF16),
            pltpu.VMEM((cap, n_lanes, tokens, head_cols), BF16),
            pltpu.VMEM((batch, span_len, head_cols), BF16),
            pltpu.VMEM((n_x, stages, n_cols, n_c, batch, half, col), BF16),
            pltpu.VMEM((n_x, stages, n_cols, batch, half, col), BF16),
            pltpu.VMEM((n_x - 1, stages, n_cols, batch, half, col), BF16),
            pltpu.VMEM((n_x - 1, stages, n_cols, batch, half, col), BF16),
            pltpu.VMEM((chip_spans, half, col), BF16),
            pltpu.VMEM((n_cols, core_spans, half, col), BF16),
            dma((6,)),
            dma((2,)),
            dma((n_lanes,)),
            dma((n_lanes,)),
            dma((cap,)),
            dma((cap, n_lanes)),
            dma((1,)),
            dma((1,)),
            dma((cap, n_lanes, n_x - 1)),
            dma((cap,)),
            dma((1,)),
            dma((n_x, stages, n_cols)),
            dma((1,)),
            dma((n_x - 1, stages, n_cols)),
            dma((1,)),
            dma((1,)),
        ],
        compiler_params=pltpu.CompilerParams(
            collective_id=0, has_side_effects=True, vmem_limit_bytes=60000000
        ),
    )(
        owners.T,
        entry_ids.T,
        queries.reshape(spans, span_len, head_cols),
        span_states.reshape(spans, span_len, width),
        store,
        w_key,
        w_value,
        w_out,
    )


def solution(mesh):
    return jax.shard_map(
        shards,
        mesh=mesh,
        in_specs=(
            P(("groups", "lanes"), ("heads", "rep")),
            P(("groups", "lanes"), None),
            P(("groups", "lanes"), ("heads", "rep"), None),
            P(("groups", "lanes"), None),
            P(("groups", "lanes"), None),
            P(None, ("heads", "rep")),
            P(None, ("heads", "rep")),
            P(("heads", "rep"), None),
        ),
        out_specs=P(("groups", "lanes", "heads", "rep"), None),
        check_vma=False,
    )
```

time: 66.7 us -> 67.6 us (1.013)
  Pallas kernels: 65.5 us -> 66.2 us
where the time goes in v1:
time: 67.6 us; the launch traced here: 67.1 us
  Pallas kernels  66.2 us (98%)
  local copies, waits for them, and re-layouts  0.97 us (1%)
    pallas_call x1, Pallas kernels, shards(): pl.pallas_call(functools.partial(fused, n_lanes, n_x, n_c, cap, n_cols),...  66.2 us

profile of v1, /device:TPU:1, one launch (start us, length us, event | category | flops | bytes accessed | tf_op | source)
XLA Modules:
  0.0 67.1 jit_solution(3527118418415963253)
XLA Ops:
  0.0 66.2 %shard_map.82 = bf16[128,4096]{1,0:T(8,128)(2,1)S(1)} custom-call(s32[2,8]{1,0:T(2,128)} %bitcast.6, s32[2,8]{1,0:T(2,128)} %bitcast.7, bf16[8,64,512]{2,1,0:T(8,128)(2,1)} %bitcast.5, bf16[8,64,896]{2,1,0:T(8,128)(2,1)} %bitcast.4, bf16[16,32,896]{2,1,0:T(8,128)(2,1)} %store_hbm.1, bf16[896,512]{1,0:T(8,128)(2,1)} %wk_hbm.1, bf16[896,512]{1,0:T(8,128)(2,1)} %wv_hbm.1, ...), custom_call_target="tpu_custom_call" | custom-call | tf_op jit(solution)/shard_map/pallas_call | solution.py:485
  66.2 1.0 %copy.10 = bf16[128,4096]{1,0:T(8,128)(2,1)} copy(bf16[128,4096]{1,0:T(8,128)(2,1)S(1)} %shard_map.82) | data formatting | bytes 2097152

commit v2 on v1

--- a/solution.py
+++ b/solution.py
@@ -239,7 +239,7 @@
         send_rank(r)
     groups = n_lanes - 1
     total = cap * groups
-    lag = min(2, groups)
+    lag = min(3, groups)
     lane_chunk = min(n_lanes, 4)
 
     def settle(r):
@@ -334,92 +334,136 @@
         lax.fori_loop(lo, hi, step, 0)
 
     own = n_x - 1
-    ready = cap // 2 - 1
+
+    up = lane // (n_lanes // 2)
+
+    def member(i):
+        g = i % groups
+        return i // groups, up * (1 + g) + (1 - up) * (n_lanes - 1 - g)
+
+    behind = min(5, n_cols)
+
+    def blend(k, e):
+        attend(k, e)
+
+        def step(j, carry):
+            @pl.when(j < n_cols)
+            def _():
+                product(k, e, j)
+
+            @pl.when(j >= behind)
+            def _():
+                combine(k, e, j - behind)
+
+            return carry
+
+        lax.fori_loop(0, n_cols + behind, step, 0)
+
+    def some_products(k, e, lo, hi):
+        def step(j, carry):
+            product(k, e, j)
+            return carry
+
+        lax.fori_loop(lo, hi, step, 0)
+
+    def relays(lo, hi):
+        def step(i, carry):
+            relay(*member(i))
+            return carry
+
+        lax.fori_loop(lo, hi, step, 0)
+
+    def own_relays():
+        for n in range(cap):
+            relay(n, 0)
+
+    def weights_here():
+        for load in loads[2:]:
+            load.wait()
+
+    soon = cap // 2 * groups
+    some = n_cols // 2
 
     def slot_step(i, carry):
-        r, d = i // groups, 1 + i % groups
+        r, d = member(i)
         tok_copy(r, d).wait_recv()
         encode([(r, d)], lambda r, d: recv_tok[r, d])
 
-        @pl.when(i == lag - 1)
-        def _():
-            for n in range(cap):
-                relay(n, 0)
-
-        @pl.when(i >= lag)
-        def _():
-            relay((i - lag) // groups, 1 + (i - lag) % groups)
-
         for n in range(ahead, cap):
 
             @pl.when(i == (n - 1) * groups - 1)
             def _():
-                toks_sent(n - ahead)
                 send_rank(n)
 
-        @pl.when(i == groups + lag - 1)
-        def _():
-            loads[2].wait()
-            loads[3].wait()
-
-        for n in range(cap - 1):
-
-            @pl.when(i == (n + 1) * groups + lag - 1)
-            def _():
-                project(n)
-                if early and n == ready:
-                    loads[4].wait()
-                    loads[5].wait()
-                    for k in range(own):
-                        products(k, 0)
-                if early and n == ready + 1:
-                    for k in range(own):
-                        combines(k, 0, 1, 2)
-
         if early:
 
-            @pl.when(i == (ready + 2) * groups)
-            def _():
-                for k in range(own):
-                    combines(k, 0, 0, 1)
+            @pl.when(i == soon - 1)
+            def _():
+                own_relays()
+
+            @pl.when(i == soon)
+            def _():
+                relays(0, 2)
+
+            @pl.when(i == soon + 1)
+            def _():
+                relays(2, groups)
+                weights_here()
+
+            @pl.when(i == soon + 2)
+            def _():
+                relays(groups, soon)
+                project(0)
+
+            @pl.when(i == soon + 3)
+            def _():
+                project(1)
+
+            @pl.when(i == soon + 4)
+            def _():
+                attend(0, 0)
+                some_products(0, 0, 0, some)
+
+            @pl.when(i == soon + 5)
+            def _():
+                combines(0, 0, 0, some // 2)
+                some_products(0, 0, some, n_cols)
+                combines(0, 0, some // 2, some)
+                relays(soon, soon + groups)
+
+        else:
+
+            @pl.when(i == lag - 1)
+            def _():
+                own_relays()
+                weights_here()
+
+            @pl.when(i >= lag)
+            def _():
+                relays(i - lag, i - lag + 1)
+
+            for n in range(cap - 1):
+
+                @pl.when(i == (n + 1) * groups + lag - 1)
+                def _():
+                    project(n)
 
         return carry
 
     lax.fori_loop(0, total, slot_step, 0)
     if early:
-        for k in range(own):
-            combines(k, 0, 2, n_cols // 2)
-        products(own, 0)
-        for k in range(own):
-            combines(k, 0, n_cols // 2, n_cols)
+        combines(0, 0, some, n_cols)
+        relays(soon + groups, total)
+        for n in range(cap // 2, cap):
+            project(n)
     else:
-        loads[4].wait()
-        loads[5].wait()
-
-    def late_relay(i, carry):
-        relay(i // groups, 1 + i % groups)
-        return carry
-
-    lax.fori_loop(total - lag, total, late_relay, 0)
-    project(cap - 1)
+        relays(total - lag, total)
+        project(cap - 1)
     last = stages - 1
-    behind = min(5, n_cols)
     for k in range(own):
-        attend(k, last)
-
-        def late(j, carry):
-            @pl.when(j < n_cols)
-            def _():
-                product(k, last, j)
-
-            @pl.when(j >= behind)
-            def _():
-                combine(k, last, j - behind)
-
-            return carry
-
-        lax.fori_loop(0, n_cols + behind, late, 0)
-    products(own, last)
+        blend(k, last)
+    for e in range(stages):
+        products(own, e)
 
     def final_copy(j, n):
         rows = pl.ds(pl.multiple_of(n * span_len + c * half, half), half)
@@ -448,7 +492,7 @@
     lax.fori_loop(0, n_cols, finish, 0)
     for d in range(1, n_lanes):
         idx_copy(d).wait_send()
-    for r in range(cap - ahead, cap):
+    for r in range(cap):
         toks_sent(r)
     sent(enc.at[:, :, pl.ds(0, n_x - 1)], x_send.at[0])
     sent(enc.at[:, :, pl.ds(0, n_x)], c_send.at[0])

time: 67.6 us -> 60.8 us (0.90)
  Pallas kernels: 66.2 us -> 59.1 us
    pallas_call x1, Pallas kernels: 66.2 us -> 59.1 us  [shards(): pl.pallas_call(functools.partial(fused, n_lanes, n_x, n_c, cap, n_cols),...]
where the time goes in v2:
time: 60.8 us; the launch traced here: 60.1 us
  Pallas kernels  59.1 us (97%)
  local copies, waits for them, and re-layouts  0.97 us (2%)
    pallas_call x1, Pallas kernels, shards(): pl.pallas_call(functools.partial(fused, n_lanes, n_x, n_c, cap, n_cols),...  59.1 us

profile of v2, /device:TPU:1, one launch (start us, length us, event | category | flops | bytes accessed | tf_op | source)
XLA Modules:
  0.0 60.1 jit_solution(8795652923008433448)
XLA Ops:
  0.0 59.1 %shard_map.82 = bf16[128,4096]{1,0:T(8,128)(2,1)S(1)} custom-call(s32[2,8]{1,0:T(2,128)} %bitcast.6, s32[2,8]{1,0:T(2,128)} %bitcast.7, bf16[8,64,512]{2,1,0:T(8,128)(2,1)} %bitcast.5, bf16[8,64,896]{2,1,0:T(8,128)(2,1)} %bitcast.4, bf16[16,32,896]{2,1,0:T(8,128)(2,1)} %store_hbm.1, bf16[896,512]{1,0:T(8,128)(2,1)} %wk_hbm.1, bf16[896,512]{1,0:T(8,128)(2,1)} %wv_hbm.1, ...), custom_call_target="tpu_custom_call" | custom-call | tf_op jit(solution)/shard_map/pallas_call | solution.py:529
  59.1 1.0 %copy.10 = bf16[128,4096]{1,0:T(8,128)(2,1)} copy(bf16[128,4096]{1,0:T(8,128)(2,1)S(1)} %shard_map.82) | data formatting | bytes 2097152

commit v3 on v2

--- a/solution.py
+++ b/solution.py
@@ -41,7 +41,7 @@
     send_tok, recv_tok, enc, keys, values, heads_out,
     part, part_in, summed, summed_in, final, final_out,
     load_sem, local_sem, idx_send, idx_recv, tok_sends, tok_recvs, x_send, c_send, x_recvs, c_recvs,
-    part_send, part_recv, sum_send, sum_recv, final_send, final_recv,
+    part_send, part_recv, own_recv, sum_send, sum_recv, early_recv, final_send, final_recv,
 ):
     lane = lax.axis_index("lanes")
     x = lax.axis_index("heads")
@@ -58,6 +58,8 @@
     quarter = x * n_c + c
     early = early_spans(n_x, n_lanes, cap, spans, fanout)
     stages = part.shape[1]
+    own = n_x - 1
+    last = stages - 1
     batch = chip_spans // stages
 
     loads = [
@@ -136,7 +138,7 @@
 
     def idx_copy(d):
         return pltpu.make_async_remote_copy(
-            src_ref=table, dst_ref=got_sm.at[lane], send_sem=idx_send.at[d], recv_sem=idx_recv.at[d],
+            src_ref=table, dst_ref=got_sm.at[lane], send_sem=idx_send.at[0], recv_sem=idx_recv.at[d - 1],
             device_id={"lanes": lax.rem(lane + d, n_lanes)}, device_id_type=MESH,
         )
 
@@ -156,7 +158,7 @@
     def tok_copy(r, d):
         return pltpu.make_async_remote_copy(
             src_ref=send_tok.at[r, d], dst_ref=recv_tok.at[r, d],
-            send_sem=tok_sends.at[r], recv_sem=tok_recvs.at[r, d],
+            send_sem=tok_sends.at[r], recv_sem=tok_recvs.at[r, d - 1],
             device_id={"lanes": lax.rem(lane + d, n_lanes)}, device_id_type=MESH,
         )
 
@@ -288,14 +290,14 @@
     def part_copy(k, e, j):
         return pltpu.make_async_remote_copy(
             src_ref=part.at[k, e, j, mate], dst_ref=part_in.at[k, e, j],
-            send_sem=part_send.at[0], recv_sem=part_recv.at[k, e, j],
+            send_sem=part_send.at[0], recv_sem=part_recv.at[k, e, j] if k < own else own_recv.at[e],
             device_id={"rep": mate}, device_id_type=MESH,
         )
 
     def sum_copy(k, e, j):
         return pltpu.make_async_remote_copy(
             src_ref=summed.at[k, e, j], dst_ref=summed_in.at[k, e, j],
-            send_sem=sum_send.at[0], recv_sem=sum_recv.at[k, e, j],
+            send_sem=sum_send.at[0], recv_sem=sum_recv.at[k, j] if e == last else early_recv.at[k],
             device_id={"heads": lax.rem(x + k + 1, n_x)}, device_id_type=MESH,
         )
 
@@ -333,7 +335,6 @@
 
         lax.fori_loop(lo, hi, step, 0)
 
-    own = n_x - 1
 
     up = lane // (n_lanes // 2)
 
@@ -422,13 +423,13 @@
             @pl.when(i == soon + 4)
             def _():
                 attend(0, 0)
+
+            @pl.when(i == soon + 5)
+            def _():
                 some_products(0, 0, 0, some)
-
-            @pl.when(i == soon + 5)
-            def _():
-                combines(0, 0, 0, some // 2)
+                combines(0, 0, 0, 1)
                 some_products(0, 0, some, n_cols)
-                combines(0, 0, some // 2, some)
+                combines(0, 0, 1, 4)
                 relays(soon, soon + groups)
 
         else:
@@ -452,14 +453,13 @@
 
     lax.fori_loop(0, total, slot_step, 0)
     if early:
-        combines(0, 0, some, n_cols)
+        combines(0, 0, 4, n_cols)
         relays(soon + groups, total)
         for n in range(cap // 2, cap):
             project(n)
     else:
         relays(total - lag, total)
         project(cap - 1)
-    last = stages - 1
     for k in range(own):
         blend(k, last)
     for e in range(stages):
@@ -475,10 +475,10 @@
 
     def finish(j, carry):
         for e in range(stages):
-            part_copy(own, e, j).wait_recv()
             total = part[own, e, j, c].astype(F32) + part_in[own, e, j].astype(F32)
             for k in range(own):
-                sum_copy(k, e, j).wait_recv()
+                if e == last:
+                    sum_copy(k, e, j).wait_recv()
                 total = total + summed_in[k, e, j].astype(F32)
             final[e * batch : (e + 1) * batch] = total.astype(BF16)
         for n in range(core_spans):
@@ -489,9 +489,17 @@
             out_ref[rows, columns(j)] = final[slot_sm[first + c * core_spans]]
         return carry
 
+    def arrived(ref, sem):
+        pltpu.make_async_remote_copy(
+            src_ref=ref, dst_ref=ref, send_sem=sem, recv_sem=sem, device_id={"rep": mate}, device_id_type=MESH
+        ).wait_recv()
+
+    for e in range(stages):
+        arrived(part_in.at[own, e], own_recv.at[e])
+    for k in range(own if last else 0):
+        arrived(summed_in.at[k, 0], early_recv.at[k])
     lax.fori_loop(0, n_cols, finish, 0)
-    for d in range(1, n_lanes):
-        idx_copy(d).wait_send()
+    sent(got_sm.at[pl.ds(0, n_lanes - 1)], idx_send.at[0])
     for r in range(cap):
         toks_sent(r)
     sent(enc.at[:, :, pl.ds(0, n_x - 1)], x_send.at[0])
@@ -560,18 +568,20 @@
             pltpu.VMEM((n_cols, core_spans, half, col), BF16),
             dma((6,)),
             dma((2,)),
-            dma((n_lanes,)),
-            dma((n_lanes,)),
+            dma((1,)),
+            dma((n_lanes - 1,)),
             dma((cap,)),
-            dma((cap, n_lanes)),
+            dma((cap, n_lanes - 1)),
             dma((1,)),
             dma((1,)),
             dma((cap, n_lanes, n_x - 1)),
             dma((cap,)),
             dma((1,)),
-            dma((n_x, stages, n_cols)),
+            dma((n_x - 1, stages, n_cols)),
+            dma((stages,)),
             dma((1,)),
-            dma((n_x - 1, stages, n_cols)),
+            dma((n_x - 1, n_cols)),
+            dma((n_x - 1,)),
             dma((1,)),
             dma((1,)),
         ],

time: 60.8 us -> 60.1 us (0.988)
  no operation moved by 1% of the time
where the time goes in v3:
time: 60.1 us; the launch traced here: 59.8 us
  Pallas kernels  58.8 us (98%)
  local copies, waits for them, and re-layouts  0.97 us (2%)
    pallas_call x1, Pallas kernels, shards(): pl.pallas_call(functools.partial(fused, n_lanes, n_x, n_c, cap, n_cols),...  58.8 us

profile of v3, /device:TPU:1, one launch (start us, length us, event | category | flops | bytes accessed | tf_op | source)
XLA Modules:
  0.0 59.8 jit_solution(14918546070456021997)
XLA Ops:
  0.0 58.8 %shard_map.82 = bf16[128,4096]{1,0:T(8,128)(2,1)S(1)} custom-call(s32[2,8]{1,0:T(2,128)} %bitcast.6, s32[2,8]{1,0:T(2,128)} %bitcast.7, bf16[8,64,512]{2,1,0:T(8,128)(2,1)} %bitcast.5, bf16[8,64,896]{2,1,0:T(8,128)(2,1)} %bitcast.4, bf16[16,32,896]{2,1,0:T(8,128)(2,1)} %store_hbm.1, bf16[896,512]{1,0:T(8,128)(2,1)} %wk_hbm.1, bf16[896,512]{1,0:T(8,128)(2,1)} %wv_hbm.1, ...), custom_call_target="tpu_custom_call" | custom-call | tf_op jit(solution)/shard_map/pallas_call | solution.py:537
  58.8 1.0 %copy.10 = bf16[128,4096]{1,0:T(8,128)(2,1)} copy(bf16[128,4096]{1,0:T(8,128)(2,1)S(1)} %shard_map.82) | data formatting | bytes 2097152

commit v4 on v3

--- a/solution.py
+++ b/solution.py
@@ -342,7 +342,7 @@
         g = i % groups
         return i // groups, up * (1 + g) + (1 - up) * (n_lanes - 1 - g)
 
-    behind = min(5, n_cols)
+    behind = min(4, n_cols)
 
     def blend(k, e):
         attend(k, e)
@@ -426,10 +426,10 @@
 
             @pl.when(i == soon + 5)
             def _():
-                some_products(0, 0, 0, some)
-                combines(0, 0, 0, 1)
-                some_products(0, 0, some, n_cols)
-                combines(0, 0, 1, 4)
+                some_products(0, 0, 0, some + 2)
+                combines(0, 0, 0, 2)
+                some_products(0, 0, some + 2, n_cols)
+                combines(0, 0, 2, 4)
                 relays(soon, soon + groups)
 
         else:

time: 60.1 us -> 60.1 us (level)
  no operation moved by 1% of the time
where the time goes in v4:
time: 60.1 us; the launch traced here: 59.8 us
  Pallas kernels  58.8 us (98%)
  local copies, waits for them, and re-layouts  0.97 us (2%)
    pallas_call x1, Pallas kernels, shards(): pl.pallas_call(functools.partial(fused, n_lanes, n_x, n_c, cap, n_cols),...  58.8 us

profile of v4, /device:TPU:1, one launch (start us, length us, event | category | flops | bytes accessed | tf_op | source)
XLA Modules:
  0.0 59.8 jit_solution(12666811101312565739)
XLA Ops:
  0.0 58.8 %shard_map.82 = bf16[128,4096]{1,0:T(8,128)(2,1)S(1)} custom-call(s32[2,8]{1,0:T(2,128)} %bitcast.6, s32[2,8]{1,0:T(2,128)} %bitcast.7, bf16[8,64,512]{2,1,0:T(8,128)(2,1)} %bitcast.5, bf16[8,64,896]{2,1,0:T(8,128)(2,1)} %bitcast.4, bf16[16,32,896]{2,1,0:T(8,128)(2,1)} %store_hbm.1, bf16[896,512]{1,0:T(8,128)(2,1)} %wk_hbm.1, bf16[896,512]{1,0:T(8,128)(2,1)} %wv_hbm.1, ...), custom_call_target="tpu_custom_call" | custom-call | tf_op jit(solution)/shard_map/pallas_call | solution.py:537
  58.8 1.0 %copy.10 = bf16[128,4096]{1,0:T(8,128)(2,1)} copy(bf16[128,4096]{1,0:T(8,128)(2,1)S(1)} %shard_map.82) | data formatting | bytes 2097152

commit v5 on v4

--- a/solution.py
+++ b/solution.py
@@ -238,7 +238,11 @@
         idx_copy(d).wait_recv()
         send_one(0, n_lanes - d)
     for r in range(1, ahead):
-        send_rank(r)
+
+        @pl.when(c == 0)
+        def _():
+            send_rank(r)
+
     groups = n_lanes - 1
     total = cap * groups
     lag = min(3, groups)
@@ -389,6 +393,12 @@
         r, d = member(i)
         tok_copy(r, d).wait_recv()
         encode([(r, d)], lambda r, d: recv_tok[r, d])
+
+        for n in range(1, ahead):
+
+            @pl.when(jnp.logical_and(i == 0, c > 0))
+            def _():
+                send_rank(n)
 
         for n in range(ahead, cap):
 

time: 60.1 us -> 60.6 us (level)
  no operation moved by 1% of the time
where the time goes in v5:
time: 60.6 us; the launch traced here: 60 us
  Pallas kernels  59 us (97%)
  local copies, waits for them, and re-layouts  0.97 us (2%)
    pallas_call x1, Pallas kernels, shards(): pl.pallas_call(functools.partial(fused, n_lanes, n_x, n_c, cap, n_cols),...  59 us

profile of v5, /device:TPU:1, one launch (start us, length us, event | category | flops | bytes accessed | tf_op | source)
XLA Modules:
  0.0 60.0 jit_solution(17063331131576235248)
XLA Ops:
  0.0 59.0 %shard_map.82 = bf16[128,4096]{1,0:T(8,128)(2,1)S(1)} custom-call(s32[2,8]{1,0:T(2,128)} %bitcast.6, s32[2,8]{1,0:T(2,128)} %bitcast.7, bf16[8,64,512]{2,1,0:T(8,128)(2,1)} %bitcast.5, bf16[8,64,896]{2,1,0:T(8,128)(2,1)} %bitcast.4, bf16[16,32,896]{2,1,0:T(8,128)(2,1)} %store_hbm.1, bf16[896,512]{1,0:T(8,128)(2,1)} %wk_hbm.1, bf16[896,512]{1,0:T(8,128)(2,1)} %wv_hbm.1, ...), custom_call_target="tpu_custom_call" | custom-call | tf_op jit(solution)/shard_map/pallas_call | solution.py:547
  59.0 1.0 %copy.10 = bf16[128,4096]{1,0:T(8,128)(2,1)} copy(bf16[128,4096]{1,0:T(8,128)(2,1)S(1)} %shard_map.82) | data formatting | bytes 2097152
